TPU v7x, 128 devices: a whole 4x4x4 slice. The times are simulated.
128 devices in a mesh: gz: 8 (over x, core), xy: 16 (over y, z).
Axes of the slice: x: 4, y: 4, z: 4, core: 2. Of those that a mesh axis runs over, the one named last changes fastest.
Arguments:
- parent_feat: bfloat16 [128, 64, 2048], P(('gz', 'xy')), may hold values from -6 to 6
- parent_cell: int32 [128, 2048], P(('gz', 'xy')), may hold values from 0 to 255
- send_count: int32 [128, 128], P(('gz', 'xy')), may hold values from 1 to 16, as said below
- up_weight: bfloat16 [8, 64, 64], replicated, may hold values from -0.75 to 0.75
- conv_one: bfloat16 [27, 64, 64], replicated, may hold values from -0.15625 to 0.15625
- conv_two: bfloat16 [27, 64, 64], replicated, may hold values from -0.15625 to 0.15625
- child_mask: int32 [32, 8, 1024], P('xy', None, 'gz'), may hold values 0 or 1
- cotangent: bfloat16 [64, 32, 8, 1024], P(None, 'xy', None, 'gz'), may hold values from -6 to 6
Outputs:
- decoded: bfloat16 [64, 32, 8, 1024], P(None, 'xy', None, 'gz')
- grad_parent: bfloat16 [128, 64, 2048], P(('gz', 'xy'))
- grad_one: float32 [27, 64, 64], replicated
- grad_two: float32 [27, 64, 64], replicated
- grad_up: float32 [8, 64, 64], replicated
Inputs may be any that keep to these rules, and one draw needn't show every extreme that they name: `send_count`: some receiver gets 16 live slots from every sender, and every sender fills all 16 slots to some receiver. `parent_cell`: several slots may name the same parent voxel; their features add.
All inputs are finite; a program needn't handle non-finite values. No bound on the sum of `child_mask` on one device may be relied on, other than what follows from the above.
Results may differ from a plain program's by a relative error of at most 0.008.
Values may be sent and summed in bfloat16 or wider, within the bound.
No kernel may reach another device: no remote copies, remote signals or barrier semaphores. Data moves between devices by JAX's collectives and lax.ppermute only.
A program may use at most 64 MiB of HBM per device.

v0:
```python
import math
import jax
import jax.numpy as jnp
from jax import lax
from jax.sharding import PartitionSpec as P

OFFSETS = [(a, b, c) for a in (-1, 0, 1) for b in (-1, 0, 1) for c in (-1, 0, 1)]


def with_halo(shard, sides, width):
    for axis, dim in sides:
        devices, length = (lax.axis_size(axis), shard.shape[dim])
        up = [(i, (i + 1) % devices) for i in range(devices - 1)]
        down = [(j, i) for i, j in up]
        last = lax.slice_in_dim(shard, length - width, length, axis=dim)
        first = lax.slice_in_dim(shard, 0, width, axis=dim)
        before = lax.ppermute(last, axis, up)
        after = lax.ppermute(first, axis, down)
        shard = jnp.concatenate([before, shard, after], axis=dim)
    return shard


def extend(field):
    bordered = with_halo(field, (("xy", 1), ("gz", 3)), 1)
    return jnp.pad(bordered, ((0, 0), (0, 0), (1, 1), (0, 0)))


def window(padded, offset, direction, shape):
    nx, ny, nz = (shape[1], shape[2], shape[3])
    ox, oy, oz = (offset[0] * direction, offset[1] * direction, offset[2] * direction)
    part = padded[:, 1 + ox : 1 + ox + nx, 1 + oy : 1 + oy + ny, 1 + oz : 1 + oz + nz]
    return part.reshape(shape[0], -1)


def orient(matrix, direction):
    return matrix if direction > 0 else matrix.T


def convolve(padded, weights, direction, shape):
    total = jnp.zeros((shape[0], shape[1] * shape[2] * shape[3]), jnp.float32)
    for index, offset in enumerate(OFFSETS):
        total = total + jnp.dot(
            orient(weights[index], direction),
            window(padded, offset, direction, shape),
            preferred_element_type=jnp.float32,
        )
    return total.reshape(shape)


def weight_terms(delta, padded, shape):
    flat = delta.reshape(shape[0], -1)
    terms = [
        lax.dot_general(
            flat,
            window(padded, offset, 1, shape),
            (((1,), (1,)), ((), ())),
            preferred_element_type=jnp.float32,
        )
        for offset in OFFSETS
    ]
    return jnp.stack(terms)


def silu_slope(value):
    sig = jax.nn.sigmoid(value)
    return sig * (1.0 + value * (1.0 - sig))


def local(
    parent_feat, parent_cell, send_count, up_weight, conv_one, conv_two, child_mask, cotangent
):
    channels, size_x, size_y, size_z = cotangent.shape
    shape = cotangent.shape
    count_gz = lax.axis_size("gz")
    count_xy = lax.axis_size("xy")
    devices_all = count_gz * count_xy
    slot_total = parent_feat.shape[2]
    capacity = slot_total // devices_all
    half_x, half_y, half_z = (size_x // 2, size_y // 2, size_z // 2)
    parent_total = half_x * half_y * half_z
    slot_pos = jnp.arange(slot_total, dtype=jnp.int32) % capacity
    live = slot_pos < jnp.repeat(send_count[0], capacity)
    feats = jnp.where(live[None, :], parent_feat[0], jnp.zeros_like(parent_feat[0]))
    got_feat, got_cell = (
        lax.all_to_all(feats, ("gz", "xy"), split_axis=1, concat_axis=1, tiled=True),
        lax.all_to_all(parent_cell, ("gz", "xy"), split_axis=1, concat_axis=1, tiled=True),
    )
    got_cell = got_cell.reshape(slot_total)
    onehot = (got_cell[:, None] == jnp.arange(parent_total, dtype=jnp.int32)[None, :]).astype(
        jnp.bfloat16
    )
    parent_grid = jnp.dot(got_feat, onehot, preferred_element_type=jnp.float32).astype(jnp.bfloat16)
    up8 = jnp.einsum("ocd,dq->ocq", up_weight, parent_grid, preferred_element_type=jnp.float32)
    up = (
        up8.reshape(2, 2, 2, channels, half_x, half_y, half_z)
        .transpose(3, 4, 0, 5, 1, 6, 2)
        .reshape(shape)
    )
    maskf = child_mask.astype(jnp.float32)
    lifted = (maskf * up).astype(jnp.bfloat16)
    lifted_pad = extend(lifted)
    first_pre = convolve(lifted_pad, conv_one, 1, shape)
    first_act = (maskf * jax.nn.silu(first_pre)).astype(jnp.bfloat16)
    first_pad = extend(first_act)
    second_pre = convolve(first_pad, conv_two, 1, shape)
    decoded = (maskf * jax.nn.silu(second_pre)).astype(jnp.bfloat16)
    delta_two = (cotangent.astype(jnp.float32) * maskf * silu_slope(second_pre)).astype(
        jnp.bfloat16
    )
    term_two = weight_terms(delta_two, first_pad, shape)
    back_one = convolve(extend(delta_two), conv_two, -1, shape)
    delta_one = (back_one * maskf * silu_slope(first_pre)).astype(jnp.bfloat16)
    term_one = weight_terms(delta_one, lifted_pad, shape)
    delta_up = (convolve(extend(delta_one), conv_one, -1, shape) * maskf).astype(jnp.bfloat16)
    du8 = (
        delta_up.reshape(channels, half_x, 2, half_y, 2, half_z, 2)
        .transpose(2, 4, 6, 0, 1, 3, 5)
        .reshape(8, channels, parent_total)
    )
    term_up = jnp.einsum("ocq,dq->ocd", du8, parent_grid, preferred_element_type=jnp.float32)
    delta_parent = jnp.einsum(
        "ocd,ocq->dq", up_weight, du8, preferred_element_type=jnp.float32
    ).astype(jnp.bfloat16)
    slot_grad = lax.dot_general(
        delta_parent, onehot, (((1,), (1,)), ((), ())), preferred_element_type=jnp.float32
    ).astype(jnp.bfloat16)
    returned = lax.all_to_all(slot_grad, ("gz", "xy"), split_axis=1, concat_axis=1, tiled=True)
    grad_parent = jnp.where(live[None, :], returned, jnp.zeros_like(returned))[None]
    sum_one, sum_two, sum_up = lax.psum((term_one, term_two, term_up), ("gz", "xy"))
    scale = 1.0 / math.sqrt(size_x * count_xy * size_y * size_z * count_gz)
    return (decoded, grad_parent, sum_one * scale, sum_two * scale, sum_up * scale)


def solution(mesh):
    placed = (
        P(("gz", "xy"), None, None),
        P(("gz", "xy"), None),
        P(("gz", "xy"), None),
        P(),
        P(),
        P(),
        P("xy", None, "gz"),
        P(None, "xy", None, "gz"),
    )
    return jax.shard_map(
        local,
        mesh=mesh,
        in_specs=placed,
        out_specs=(P(None, "xy", None, "gz"), P(("gz", "xy"), None, None), P(), P(), P()),
        check_vma=False,
    )
```

profile of v0, /device:TPU:1, one launch (start us, length us, event | category | flops | bytes accessed | tf_op | source)
XLA Modules:
  0.0 432.3 jit_solution(10108309760339999828)
XLA Ops:
  9.8 11.5 %all-to-all-start.1 = ((s32[1,128,16]{2,0,1:T(1,128)}), s32[1,128,16]{2,0,1:T(1,128)S(1)}, u32[]{:S(2)}, u32[]{:S(2)}) async-start(s32[1,128,16]{2,0,1:T(1,128)} %bitcast.3), calls=%async_computation.1 | async-start | bytes 131072 | tf_op jit(solution)/shard_map/all_to_all | solution.py:86
  24.6 6.2 %all-to-all-done.1 = s32[1,128,16]{2,0,1:T(1,128)S(1)} async-done(((s32[1,128,16]{2,0,1:T(1,128)}), s32[1,128,16]{2,0,1:T(1,128)S(1)}, u32[]{:S(2)}, u32[]{:S(2)}) %all-to-all-start.1) | async-done | bytes 8224 | tf_op jit(solution)/shard_map/all_to_all | solution.py:86
  30.8 4.5 %all-to-all-start = ((bf16[128,2,512]{2,1,0:T(2,128)(2,1)}), bf16[128,2,512]{2,1,0:T(2,128)(2,1)S(1)}, u32[]{:S(2)}, u32[]{:S(2)}) async-start(bf16[128,2,512]{2,1,0:T(2,128)(2,1)} %reshape.685), calls=%async_computation | async-start | bytes 524288 | tf_op jit(solution)/shard_map/all_to_all | solution.py:85
  36.8 9.8 %all-to-all-done = bf16[128,2,512]{2,1,0:T(2,128)(2,1)S(1)} async-done(((bf16[128,2,512]{2,1,0:T(2,128)(2,1)}), bf16[128,2,512]{2,1,0:T(2,128)(2,1)S(1)}, u32[]{:S(2)}, u32[]{:S(2)}) %all-to-all-start) | async-done | bytes 262176 | tf_op jit(solution)/shard_map/all_to_all | solution.py:85
  49.3 2.5 collective-permute-start
  53.9 3.6 collective-permute-done.1
  57.8 4.3 collective-permute-start.2
  62.1 1.9 collective-permute-start.3
  65.7 2.5 collective-permute-done.2
  68.2 4.4 %collective-permute-done.3 = bf16[64,4,8,1]{3,0,2,1:T(8,128)(2,1)S(1)} collective-permute-done((bf16[64,4,8,1]{3,0,2,1:T(8,128)(2,1)S(1)}, bf16[64,4,8,1]{3,0,2,1:T(8,128)(2,1)S(1)}, u32[]{:S(2)}, u32[]{:S(2)}) %collective-permute-start.3) | collective-permute-done | bytes 4128 | tf_op jit(solution)/shard_map/ppermute | solution.py:18
  92.9 2.0 collective-permute-start.4
  96.8 3.8 collective-permute-done.5
  102.5 4.1 collective-permute-start.6
  106.7 2.5 collective-permute-start.7
  110.8 2.3 collective-permute-done.6
  113.1 4.4 %collective-permute-done.7 = bf16[64,4,8,1]{3,0,2,1:T(8,128)(2,1)} collective-permute-done((bf16[64,4,8,1]{3,0,2,1:T(8,128)(2,1)}, bf16[64,4,8,1]{3,0,2,1:T(8,128)(2,1)}, u32[]{:S(2)}, u32[]{:S(2)}) %collective-permute-start.7) | collective-permute-done | bytes 4128 | tf_op jit(solution)/shard_map/ppermute | solution.py:18
  149.3 5.2 %collective-permute-start.8 = (bf16[64,1,8,128]{3,0,2,1:T(8,128)(2,1)S(1)}, bf16[64,1,8,128]{3,0,2,1:T(8,128)(2,1)S(1)}, u32[]{:S(2)}, u32[]{:S(2)}) collective-permute-start(bf16[64,1,8,128]{3,0,2,1:T(8,128)(2,1)S(1)} %get-tuple-element.144), channel_id=1, source_target_pairs={{0,1},{1,2},{2,3},{3,4},{4,5},{5,6},{6,7},{7,8},{8,9},{9,10},{10,1... | collective-permute-start | bytes 393224 | tf_op jit(solution)/shard_map/ppermute | solution.py:17
  156.4 3.8 collective-permute-done.9
  160.6 3.8 collective-permute-start.10
  164.4 1.9 collective-permute-start.11
  166.8 3.7 collective-permute-done.10
  170.5 4.4 %collective-permute-done.11 = bf16[64,4,8,1]{3,0,2,1:T(8,128)(2,1)S(1)} collective-permute-done((bf16[64,4,8,1]{3,0,2,1:T(8,128)(2,1)S(1)}, bf16[64,4,8,1]{3,0,2,1:T(8,128)(2,1)S(1)}, u32[]{:S(2)}, u32[]{:S(2)}) %collective-permute-start.11) | collective-permute-done | bytes 4128 | tf_op jit(solution)/shard_map/ppermute | solution.py:18
  203.5 3.5 collective-permute-start.12
  208.9 3.8 collective-permute-done.13
  213.0 4.1 collective-permute-start.14
  217.2 1.9 collective-permute-start.15
  219.4 3.9 collective-permute-done.14
  223.3 4.4 %collective-permute-done.15 = bf16[64,4,8,1]{3,0,2,1:T(8,128)(2,1)S(1)} collective-permute-done((bf16[64,4,8,1]{3,0,2,1:T(8,128)(2,1)S(1)}, bf16[64,4,8,1]{3,0,2,1:T(8,128)(2,1)S(1)}, u32[]{:S(2)}, u32[]{:S(2)}) %collective-permute-start.15) | collective-permute-done | bytes 4128 | tf_op jit(solution)/shard_map/ppermute | solution.py:18
  253.7 7.1 %all-to-all-start.2 = ((bf16[128,2,512]{2,1,0:T(2,128)(2,1)}), bf16[128,2,512]{2,1,0:T(2,128)(2,1)S(1)}, u32[]{:S(2)}, u32[]{:S(2)}) async-start(bf16[128,2,512]{2,1,0:T(2,128)(2,1)} %reshape.687), calls=%async_computation.2 | async-start | bytes 524288 | tf_op jit(solution)/shard_map/all_to_all | solution.py:127
  262.7 9.3 %all-to-all-done.2 = bf16[128,2,512]{2,1,0:T(2,128)(2,1)S(1)} async-done(((bf16[128,2,512]{2,1,0:T(2,128)(2,1)}), bf16[128,2,512]{2,1,0:T(2,128)(2,1)S(1)}, u32[]{:S(2)}, u32[]{:S(2)}) %all-to-all-start.2) | async-done | bytes 262176 | tf_op jit(solution)/shard_map/all_to_all | solution.py:127
  273.6 147.1 %all-reduce.7.cloned.1.call-done = (f32[27,64,64]{2,1,0:T(8,128)}, f32[27,64,64]{2,1,0:T(8,128)}, f32[8,64,64]{2,1,0:T(8,128)}) async-done(((f32[27,64,64]{2,1,0:T(8,128)}, f32[27,64,64]{2,1,0:T(8,128)}, f32[8,64,64]{2,1,0:T(8,128)}), (f32[27,64,64]{2,1,0:T(8,128)}, f32[27,64,64]{2,1,0:T(8,128)}, f32[8,64,64]{2,1,0:T(8,128)})) %all-reduce.7.cloned.1.call-update) | async-done | bytes 1015824 | tf_op jit(solution)/shard_map/psum | solution.py:129
  422.4 2.9 broadcast_multiply_fusion
  (421 shorter events, 134.7 us)
Async XLA Ops:
  7.2 40.4 %copy-start = (bf16[8,64,64]{2,1,0:T(8,128)(2,1)S(1)}, bf16[8,64,64]{2,1,0:T(8,128)(2,1)}, u32[]{:S(2)}) copy-start(bf16[8,64,64]{2,1,0:T(8,128)(2,1)} %param.11) | copy-start | bytes 196612
  9.8 21.0 %all-to-all-start.1 = ((s32[1,128,16]{2,0,1:T(1,128)}), s32[1,128,16]{2,0,1:T(1,128)S(1)}, u32[]{:S(2)}, u32[]{:S(2)}) async-start(s32[1,128,16]{2,0,1:T(1,128)} %bitcast.3), calls=%async_computation.1 | async-start | bytes 131072 | tf_op jit(solution)/shard_map/all_to_all | solution.py:86
  23.2 12.0 %copy-start.33 = (s32[2,8,128]{2,1,0:T(8,128)S(1)}, s32[2,8,128]{2,1,0:T(8,128)}, u32[]{:S(2)}) copy-start(s32[2,8,128]{2,1,0:T(8,128)} %param.14) | copy-start | bytes 24580
  30.8 15.7 %all-to-all-start = ((bf16[128,2,512]{2,1,0:T(2,128)(2,1)}), bf16[128,2,512]{2,1,0:T(2,128)(2,1)S(1)}, u32[]{:S(2)}, u32[]{:S(2)}) async-start(bf16[128,2,512]{2,1,0:T(2,128)(2,1)} %reshape.685), calls=%async_computation | async-start | bytes 524288 | tf_op jit(solution)/shard_map/all_to_all | solution.py:85
  36.8 10.1 %copy-start.34 = (s32[2048]{0:T(1024)}, s32[2048]{0:T(1024)S(1)}, u32[]{:S(2)}) copy-start(s32[2048]{0:T(1024)S(1)} %eq.17) | copy-start | bytes 24580
  49.3 4.6 %collective-permute-start = (bf16[64,1,8,128]{3,0,2,1:T(8,128)(2,1)S(1)}, bf16[64,1,8,128]{3,0,2,1:T(8,128)(2,1)S(1)}, u32[]{:S(2)}, u32[]{:S(2)}) collective-permute-start(bf16[64,1,8,128]{3,0,2,1:T(8,128)(2,1)S(1)} %get-tuple-element.148), channel_id=1, source_target_pairs={{0,1},{1,2},{2,3},{3,4},{4,5},{5,6},{6,7},{7,8},{8,9},{9,10},{10,1... | collective-permute-start | bytes 393224 | tf_op jit(solution)/shard_map/ppermute | solution.py:17
  51.8 5.7 %collective-permute-start.1 = (bf16[64,1,8,128]{3,0,2,1:T(8,128)(2,1)S(1)}, bf16[64,1,8,128]{3,0,2,1:T(8,128)(2,1)S(1)}, u32[]{:S(2)}, u32[]{:S(2)}) collective-permute-start(bf16[64,1,8,128]{3,0,2,1:T(8,128)(2,1)S(1)} %get-tuple-element.149), channel_id=1, source_target_pairs={{1,0},{2,1},{3,2},{4,3},{5,4},{6,5},{7,6},{8,7},{9,8},{10,9},{11,1... | collective-permute-start | bytes 393224 | tf_op jit(solution)/shard_map/ppermute | solution.py:18
  53.6 10.4 %copy-start.1 = (f32[2,4,2,64,2]{4,3,2,1,0:T(8,128)}, f32[2,4,2,64,2]{4,3,2,1,0:T(8,128)S(1)}, u32[]{:S(2)}) copy-start(f32[2,4,2,64,2]{4,3,2,1,0:T(8,128)S(1)} %mul.119) | copy-start | bytes 24580
  53.9 18.7 %copy-start.17 = (bf16[64,1,8,128]{3,0,2,1:T(8,128)(2,1)}, bf16[64,1,8,128]{3,0,2,1:T(8,128)(2,1)S(1)}, u32[]{:S(2)}) copy-start(bf16[64,1,8,128]{3,0,2,1:T(8,128)(2,1)S(1)} %collective-permute-done) | copy-start | bytes 393220
  57.8 10.4 %collective-permute-start.2 = (bf16[64,4,8,1]{3,0,2,1:T(8,128)(2,1)S(1)}, bf16[64,4,8,1]{3,0,2,1:T(8,128)(2,1)S(1)}, u32[]{:S(2)}, u32[]{:S(2)}) collective-permute-start(bf16[64,4,8,1]{3,0,2,1:T(8,128)(2,1)S(1)} %get-tuple-element.132), channel_id=1, source_target_pairs={{0,16},{16,32},{32,48},{48,64},{64,80},{80,96},{96,112},{1,17},{17... | collective-permute-start | bytes 12296 | tf_op jit(solution)/shard_map/ppermute | solution.py:17
  62.1 10.5 %collective-permute-start.3 = (bf16[64,4,8,1]{3,0,2,1:T(8,128)(2,1)S(1)}, bf16[64,4,8,1]{3,0,2,1:T(8,128)(2,1)S(1)}, u32[]{:S(2)}, u32[]{:S(2)}) collective-permute-start(bf16[64,4,8,1]{3,0,2,1:T(8,128)(2,1)S(1)} %get-tuple-element.133), channel_id=1, source_target_pairs={{16,0},{32,16},{48,32},{64,48},{80,64},{96,80},{112,96},{17,1},{33... | collective-permute-start | bytes 12296 | tf_op jit(solution)/shard_map/ppermute | solution.py:18
  77.2 10.4 %copy-start.3 = (bf16[64,2,8,128]{3,0,2,1:T(8,128)(2,1)}, bf16[64,2,8,128]{3,0,2,1:T(8,128)(2,1)S(1)}, u32[]{:S(2)}) copy-start(bf16[64,2,8,128]{3,0,2,1:T(8,128)(2,1)S(1)} %get-tuple-element.120) | copy-start | bytes 786436
  77.2 10.8 %copy-start.5 = (bf16[64,2,8,128]{3,0,2,1:T(8,128)(2,1)}, bf16[64,2,8,128]{3,0,2,1:T(8,128)(2,1)S(1)}, u32[]{:S(2)}) copy-start(bf16[64,2,8,128]{3,0,2,1:T(8,128)(2,1)S(1)} %get-tuple-element.141) | copy-start | bytes 786436
  92.9 3.9 collective-permute-start.4
  94.9 5.7 %collective-permute-start.5 = (bf16[64,1,8,128]{3,0,2,1:T(8,128)(2,1)S(1)}, bf16[64,1,8,128]{3,0,2,1:T(8,128)(2,1)S(1)}, u32[]{:S(2)}, u32[]{:S(2)}) collective-permute-start(bf16[64,1,8,128]{3,0,2,1:T(8,128)(2,1)S(1)} %get-tuple-element.147), channel_id=1, source_target_pairs={{1,0},{2,1},{3,2},{4,3},{5,4},{6,5},{7,6},{8,7},{9,8},{10,9},{11,1... | collective-permute-start | bytes 393224 | tf_op jit(solution)/shard_map/ppermute | solution.py:18
  96.8 3.8 copy-start.19
  101.4 7.8 %copy-start.36 = (s32[1,128]{1,0:T(1,128)S(1)}, s32[1,128]{1,0:T(1,128)}, u32[]{:S(2)}) copy-start(s32[1,128]{1,0:T(1,128)} %param.10) | copy-start | bytes 1540
  102.5 10.6 %collective-permute-start.6 = (bf16[64,4,8,1]{3,0,2,1:T(8,128)(2,1)}, bf16[64,4,8,1]{3,0,2,1:T(8,128)(2,1)}, u32[]{:S(2)}, u32[]{:S(2)}) collective-permute-start(bf16[64,4,8,1]{3,0,2,1:T(8,128)(2,1)} %get-tuple-element.130), channel_id=1, source_target_pairs={{0,16},{16,32},{32,48},{48,64},{64,80},{80,96},{96,112},{1,17},{17... | collective-permute-start | bytes 12296 | tf_op jit(solution)/shard_map/ppermute | solution.py:17
  106.7 10.8 %collective-permute-start.7 = (bf16[64,4,8,1]{3,0,2,1:T(8,128)(2,1)}, bf16[64,4,8,1]{3,0,2,1:T(8,128)(2,1)}, u32[]{:S(2)}, u32[]{:S(2)}) collective-permute-start(bf16[64,4,8,1]{3,0,2,1:T(8,128)(2,1)} %get-tuple-element.131), channel_id=1, source_target_pairs={{16,0},{32,16},{48,32},{64,48},{80,64},{96,80},{112,96},{17,1},{33... | collective-permute-start | bytes 12296 | tf_op jit(solution)/shard_map/ppermute | solution.py:18
  149.3 7.2 %collective-permute-start.8 = (bf16[64,1,8,128]{3,0,2,1:T(8,128)(2,1)S(1)}, bf16[64,1,8,128]{3,0,2,1:T(8,128)(2,1)S(1)}, u32[]{:S(2)}, u32[]{:S(2)}) collective-permute-start(bf16[64,1,8,128]{3,0,2,1:T(8,128)(2,1)S(1)} %get-tuple-element.144), channel_id=1, source_target_pairs={{0,1},{1,2},{2,3},{3,4},{4,5},{5,6},{6,7},{7,8},{8,9},{9,10},{10,1... | collective-permute-start | bytes 393224 | tf_op jit(solution)/shard_map/ppermute | solution.py:17
  154.5 5.7 %collective-permute-start.9 = (bf16[64,1,8,128]{3,0,2,1:T(8,128)(2,1)S(1)}, bf16[64,1,8,128]{3,0,2,1:T(8,128)(2,1)S(1)}, u32[]{:S(2)}, u32[]{:S(2)}) collective-permute-start(bf16[64,1,8,128]{3,0,2,1:T(8,128)(2,1)S(1)} %get-tuple-element.145), channel_id=1, source_target_pairs={{1,0},{2,1},{3,2},{4,3},{5,4},{6,5},{7,6},{8,7},{9,8},{10,9},{11,1... | collective-permute-start | bytes 393224 | tf_op jit(solution)/shard_map/ppermute | solution.py:18
  160.6 9.9 %collective-permute-start.10 = (bf16[64,4,8,1]{3,0,2,1:T(8,128)(2,1)S(1)}, bf16[64,4,8,1]{3,0,2,1:T(8,128)(2,1)S(1)}, u32[]{:S(2)}, u32[]{:S(2)}) collective-permute-start(bf16[64,4,8,1]{3,0,2,1:T(8,128)(2,1)S(1)} %get-tuple-element.128), channel_id=1, source_target_pairs={{0,16},{16,32},{32,48},{48,64},{64,80},{80,96},{96,112},{1,17},{17... | collective-permute-start | bytes 12296 | tf_op jit(solution)/shard_map/ppermute | solution.py:17
  164.4 10.5 %collective-permute-start.11 = (bf16[64,4,8,1]{3,0,2,1:T(8,128)(2,1)S(1)}, bf16[64,4,8,1]{3,0,2,1:T(8,128)(2,1)S(1)}, u32[]{:S(2)}, u32[]{:S(2)}) collective-permute-start(bf16[64,4,8,1]{3,0,2,1:T(8,128)(2,1)S(1)} %get-tuple-element.129), channel_id=1, source_target_pairs={{16,0},{32,16},{48,32},{64,48},{80,64},{96,80},{112,96},{17,1},{33... | collective-permute-start | bytes 12296 | tf_op jit(solution)/shard_map/ppermute | solution.py:18
  166.6 3.9 copy-start.27
  203.5 5.4 %collective-permute-start.12 = (bf16[64,1,8,128]{3,0,2,1:T(8,128)(2,1)S(1)}, bf16[64,1,8,128]{3,0,2,1:T(8,128)(2,1)S(1)}, u32[]{:S(2)}, u32[]{:S(2)}) collective-permute-start(bf16[64,1,8,128]{3,0,2,1:T(8,128)(2,1)S(1)} %get-tuple-element.142), channel_id=1, source_target_pairs={{0,1},{1,2},{2,3},{3,4},{4,5},{5,6},{6,7},{7,8},{8,9},{9,10},{10,1... | collective-permute-start | bytes 393224 | tf_op jit(solution)/shard_map/ppermute | solution.py:17
  207.0 5.7 %collective-permute-start.13 = (bf16[64,1,8,128]{3,0,2,1:T(8,128)(2,1)S(1)}, bf16[64,1,8,128]{3,0,2,1:T(8,128)(2,1)S(1)}, u32[]{:S(2)}, u32[]{:S(2)}) collective-permute-start(bf16[64,1,8,128]{3,0,2,1:T(8,128)(2,1)S(1)} %get-tuple-element.143), channel_id=1, source_target_pairs={{1,0},{2,1},{3,2},{4,3},{5,4},{6,5},{7,6},{8,7},{9,8},{10,9},{11,1... | collective-permute-start | bytes 393224 | tf_op jit(solution)/shard_map/ppermute | solution.py:18
  213.0 10.2 %collective-permute-start.14 = (bf16[64,4,8,1]{3,0,2,1:T(8,128)(2,1)S(1)}, bf16[64,4,8,1]{3,0,2,1:T(8,128)(2,1)S(1)}, u32[]{:S(2)}, u32[]{:S(2)}) collective-permute-start(bf16[64,4,8,1]{3,0,2,1:T(8,128)(2,1)S(1)} %get-tuple-element.126), channel_id=1, source_target_pairs={{0,16},{16,32},{32,48},{48,64},{64,80},{80,96},{96,112},{1,17},{17... | collective-permute-start | bytes 12296 | tf_op jit(solution)/shard_map/ppermute | solution.py:17
  217.2 10.5 %collective-permute-start.15 = (bf16[64,4,8,1]{3,0,2,1:T(8,128)(2,1)S(1)}, bf16[64,4,8,1]{3,0,2,1:T(8,128)(2,1)S(1)}, u32[]{:S(2)}, u32[]{:S(2)}) collective-permute-start(bf16[64,4,8,1]{3,0,2,1:T(8,128)(2,1)S(1)} %get-tuple-element.127), channel_id=1, source_target_pairs={{16,0},{32,16},{48,32},{64,48},{80,64},{96,80},{112,96},{17,1},{33... | collective-permute-start | bytes 12296 | tf_op jit(solution)/shard_map/ppermute | solution.py:18
  219.4 8.9 %copy-start.28 = (f32[27,64,64]{2,1,0:T(8,128)}, f32[27,64,64]{2,1,0:T(8,128)S(1)}, u32[]{:S(2)}) copy-start(f32[27,64,64]{2,1,0:T(8,128)S(1)} %fusion.92) | copy-start | bytes 1327108
  252.5 8.4 %copy-start.31 = (bf16[64,256,1]{1,0,2:T(8,128)(2,1)S(1)}, bf16[64,256,1]{1,0,2:T(8,128)(2,1)}, u32[]{:S(2)}) copy-start(bf16[64,256,1]{1,0,2:T(8,128)(2,1)} %copy-done.30) | copy-start | bytes 98308
  253.7 18.3 %all-to-all-start.2 = ((bf16[128,2,512]{2,1,0:T(2,128)(2,1)}), bf16[128,2,512]{2,1,0:T(2,128)(2,1)S(1)}, u32[]{:S(2)}, u32[]{:S(2)}) async-start(bf16[128,2,512]{2,1,0:T(2,128)(2,1)} %reshape.687), calls=%async_computation.2 | async-start | bytes 524288 | tf_op jit(solution)/shard_map/all_to_all | solution.py:127
  260.8 159.9 %all-reduce.7.cloned.1.call-start = ((), (), s32[]{:S(2)}) async-start(), calls=%async_computation.3 | async-start | bytes 4063232 | tf_op jit(solution)/shard_map/psum | solution.py:129
  (25 other events, 28.2 us)
Sparse Core Ops, SparseCore 0:
  267.6 153.0 all-reduce.6
where the time goes:
time: 441 us; the launch traced here: 432 us
  waiting for transfers between devices  219 us (50%)
  starting transfers between devices  66 us (15%)
  matrix products  65.7 us (15%)
  local copies, waits for them, and re-layouts  41.5 us (9%)
  other arithmetic  23.5 us (5%)
  between operations  16.7 us (4%)
    psum x1, waiting for transfers between devices, local(): lax.psum((term_one, term_two, term_up), ('gz', 'xy'))  147 us
    dot_general x108, matrix products, convolve(): jnp.dot(orient(weights[index], direction), window(padded, offset, directi...  50.1 us
    ppermute x8, waiting for transfers between devices, with_halo(): after = lax.ppermute(first, axis, down)  32.5 us
    ppermute x8, starting transfers between devices, with_halo(): before = lax.ppermute(last, axis, up)  29.5 us
    slice x108, local copies, waits for them, and re-layouts, window(): part = padded[:, 1 + ox:1 + ox + nx, 1 + oy:1 + oy + ny, 1 + oz:1 + oz + nz]  23.1 us
    ppermute x8, waiting for transfers between devices, with_halo(): before = lax.ppermute(last, axis, up)  13.9 us
    ppermute x8, starting transfers between devices, with_halo(): after = lax.ppermute(first, axis, down)  13.4 us
    dot_general x54, matrix products, weight_terms(): lax.dot_general(flat, window(padded, offset, 1, shape), (((1,), (1,)), ((...  13.2 us
  transfers between devices with their start and end apart: 20, of which 20 were waited for; matrix products, arithmetic and copies ran while one was open for 3% of the time, Pallas kernels for 0%

commit v1 on v0

--- a/solution.py
+++ b/solution.py
@@ -5,6 +5,11 @@
 from jax.sharding import PartitionSpec as P
 
 OFFSETS = [(a, b, c) for a in (-1, 0, 1) for b in (-1, 0, 1) for c in (-1, 0, 1)]
+
+
+def axis_by_axis(value_2, leading, second):
+    inner = lax.psum(value_2, leading)
+    return lax.psum(inner, second)
 
 
 def with_halo(shard, sides, width):
@@ -126,7 +131,7 @@
     ).astype(jnp.bfloat16)
     returned = lax.all_to_all(slot_grad, ("gz", "xy"), split_axis=1, concat_axis=1, tiled=True)
     grad_parent = jnp.where(live[None, :], returned, jnp.zeros_like(returned))[None]
-    sum_one, sum_two, sum_up = lax.psum((term_one, term_two, term_up), ("gz", "xy"))
+    sum_one, sum_two, sum_up = axis_by_axis((term_one, term_two, term_up), "xy", "gz")
     scale = 1.0 / math.sqrt(size_x * count_xy * size_y * size_z * count_gz)
     return (decoded, grad_parent, sum_one * scale, sum_two * scale, sum_up * scale)
 

time: 441 us -> 423 us (0.959)
  the two profiles are of different devices: /device:TPU:1 before, /device:TPU:0 now
where the time goes in v1:
time: 423 us; the launch traced here: 415 us
  waiting for transfers between devices  197 us (47%)
  starting transfers between devices  80.4 us (19%)
  matrix products  65.8 us (16%)
  local copies, waits for them, and re-layouts  36.6 us (9%)
  other arithmetic  18.7 us (4%)
  between operations  16.4 us (4%)
    psum x1, waiting for transfers between devices, axis_by_axis(): inner = lax.psum(value_2, leading)  83.2 us
    psum x1, waiting for transfers between devices, axis_by_axis(): return lax.psum(inner, second)  65 us
    dot_general x108, matrix products, convolve(): jnp.dot(orient(weights[index], direction), window(padded, offset, directi...  50.2 us
    ppermute x8, starting transfers between devices, with_halo(): before = lax.ppermute(last, axis, up)  38.7 us
    ppermute x8, waiting for transfers between devices, with_halo(): after = lax.ppermute(first, axis, down)  29 us
    slice x108, local copies, waits for them, and re-layouts, window(): part = padded[:, 1 + ox:1 + ox + nx, 1 + oy:1 + oy + ny, 1 + oz:1 + oz + nz]  23.1 us
    all_to_all x1, starting transfers between devices, local(): lax.all_to_all(slot_grad, ('gz', 'xy'), split_axis=1, concat_axis=1, tile...  14.9 us
    dot_general x54, matrix products, weight_terms(): lax.dot_general(flat, window(padded, offset, 1, shape), (((1,), (1,)), ((...  13.2 us
  transfers between devices with their start and end apart: 21, of which 16 were waited for; matrix products, arithmetic and copies ran while one was open for 3% of the time, Pallas kernels for 0%

profile of v1, /device:TPU:0, one launch (start us, length us, event | category | flops | bytes accessed | tf_op | source)
XLA Modules:
  0.0 415.0 jit_solution(15277234358369274785)
XLA Ops:
  7.7 1.4 reduce.6
  9.8 11.2 %all-to-all-start.1 = ((s32[1,128,16]{2,0,1:T(1,128)}), s32[1,128,16]{2,0,1:T(1,128)S(1)}, u32[]{:S(2)}, u32[]{:S(2)}) async-start(s32[1,128,16]{2,0,1:T(1,128)} %bitcast.3), calls=%async_computation.1 | async-start | bytes 131072 | tf_op jit(solution)/shard_map/all_to_all | solution.py:91
  24.3 6.1 %all-to-all-done.1 = s32[1,128,16]{2,0,1:T(1,128)S(1)} async-done(((s32[1,128,16]{2,0,1:T(1,128)}), s32[1,128,16]{2,0,1:T(1,128)S(1)}, u32[]{:S(2)}, u32[]{:S(2)}) %all-to-all-start.1) | async-done | bytes 8224 | tf_op jit(solution)/shard_map/all_to_all | solution.py:91
  30.4 4.6 %all-to-all-start = ((bf16[128,2,512]{2,1,0:T(2,128)(2,1)}), bf16[128,2,512]{2,1,0:T(2,128)(2,1)S(1)}, u32[]{:S(2)}, u32[]{:S(2)}) async-start(bf16[128,2,512]{2,1,0:T(2,128)(2,1)} %reshape.685), calls=%async_computation | async-start | bytes 524288 | tf_op jit(solution)/shard_map/all_to_all | solution.py:90
  36.0 9.9 %all-to-all-done = bf16[128,2,512]{2,1,0:T(2,128)(2,1)S(1)} async-done(((bf16[128,2,512]{2,1,0:T(2,128)(2,1)}), bf16[128,2,512]{2,1,0:T(2,128)(2,1)S(1)}, u32[]{:S(2)}, u32[]{:S(2)}) %all-to-all-start) | async-done | bytes 262176 | tf_op jit(solution)/shard_map/all_to_all | solution.py:90
  48.6 2.7 collective-permute-start
  51.4 1.3 collective-permute-start.1
  54.1 4.2 %collective-permute-done.1 = bf16[64,1,8,128]{3,0,2,1:T(8,128)(2,1)S(1)} collective-permute-done((bf16[64,1,8,128]{3,0,2,1:T(8,128)(2,1)S(1)}, bf16[64,1,8,128]{3,0,2,1:T(8,128)(2,1)S(1)}, u32[]{:S(2)}, u32[]{:S(2)}) %collective-permute-start.1) | collective-permute-done | bytes 131104 | tf_op jit(solution)/shard_map/ppermute | solution.py:23
  58.6 1.3 collective-permute-start.2
  61.2 1.7 fusion.118
  62.9 1.6 collective-permute-done.3
  83.8 2.3 collective-permute-start.4
  86.0 1.3 collective-permute-start.5
  88.5 4.4 %collective-permute-done.5 = bf16[64,1,8,128]{3,0,2,1:T(8,128)(2,1)S(1)} collective-permute-done((bf16[64,1,8,128]{3,0,2,1:T(8,128)(2,1)S(1)}, bf16[64,1,8,128]{3,0,2,1:T(8,128)(2,1)S(1)}, u32[]{:S(2)}, u32[]{:S(2)}) %collective-permute-start.5) | collective-permute-done | bytes 131104 | tf_op jit(solution)/shard_map/ppermute | solution.py:23
  93.2 7.7 %collective-permute-start.6 = (bf16[64,4,8,1]{3,0,2,1:T(8,128)(2,1)S(1)}, bf16[64,4,8,1]{3,0,2,1:T(8,128)(2,1)S(1)}, u32[]{:S(2)}, u32[]{:S(2)}) collective-permute-start(bf16[64,4,8,1]{3,0,2,1:T(8,128)(2,1)S(1)} %get-tuple-element.133), channel_id=1, source_target_pairs={{0,16},{16,32},{32,48},{48,64},{64,80},{80,96},{96,112},{1,17},{17... | collective-permute-start | bytes 12296 | tf_op jit(solution)/shard_map/ppermute | solution.py:22
  100.9 1.9 collective-permute-start.7
  102.8 3.6 collective-permute-done.7
  133.3 5.5 %collective-permute-start.8 = (bf16[64,1,8,128]{3,0,2,1:T(8,128)(2,1)S(1)}, bf16[64,1,8,128]{3,0,2,1:T(8,128)(2,1)S(1)}, u32[]{:S(2)}, u32[]{:S(2)}) collective-permute-start(bf16[64,1,8,128]{3,0,2,1:T(8,128)(2,1)S(1)} %get-tuple-element.147), channel_id=1, source_target_pairs={{0,1},{1,2},{2,3},{3,4},{4,5},{5,6},{6,7},{7,8},{8,9},{9,10},{10,1... | collective-permute-start | bytes 393224 | tf_op jit(solution)/shard_map/ppermute | solution.py:22
  141.3 4.4 %collective-permute-done.9 = bf16[64,1,8,128]{3,0,2,1:T(8,128)(2,1)S(1)} collective-permute-done((bf16[64,1,8,128]{3,0,2,1:T(8,128)(2,1)S(1)}, bf16[64,1,8,128]{3,0,2,1:T(8,128)(2,1)S(1)}, u32[]{:S(2)}, u32[]{:S(2)}) %collective-permute-start.9) | collective-permute-done | bytes 131104 | tf_op jit(solution)/shard_map/ppermute | solution.py:23
  146.0 7.7 %collective-permute-start.10 = (bf16[64,4,8,1]{3,0,2,1:T(8,128)(2,1)S(1)}, bf16[64,4,8,1]{3,0,2,1:T(8,128)(2,1)S(1)}, u32[]{:S(2)}, u32[]{:S(2)}) collective-permute-start(bf16[64,4,8,1]{3,0,2,1:T(8,128)(2,1)S(1)} %get-tuple-element.131), channel_id=1, source_target_pairs={{0,16},{16,32},{32,48},{48,64},{64,80},{80,96},{96,112},{1,17},{17... | collective-permute-start | bytes 12296 | tf_op jit(solution)/shard_map/ppermute | solution.py:22
  153.7 1.3 collective-permute-start.11
  156.2 2.6 collective-permute-done.11
  187.1 3.8 collective-permute-start.12
  193.4 4.4 %collective-permute-done.13 = bf16[64,1,8,128]{3,0,2,1:T(8,128)(2,1)S(1)} collective-permute-done((bf16[64,1,8,128]{3,0,2,1:T(8,128)(2,1)S(1)}, bf16[64,1,8,128]{3,0,2,1:T(8,128)(2,1)S(1)}, u32[]{:S(2)}, u32[]{:S(2)}) %collective-permute-start.13) | collective-permute-done | bytes 131104 | tf_op jit(solution)/shard_map/ppermute | solution.py:23
  198.0 7.7 %collective-permute-start.14 = (bf16[64,4,8,1]{3,0,2,1:T(8,128)(2,1)S(1)}, bf16[64,4,8,1]{3,0,2,1:T(8,128)(2,1)S(1)}, u32[]{:S(2)}, u32[]{:S(2)}) collective-permute-start(bf16[64,4,8,1]{3,0,2,1:T(8,128)(2,1)S(1)} %get-tuple-element.129), channel_id=1, source_target_pairs={{0,16},{16,32},{32,48},{48,64},{64,80},{80,96},{96,112},{1,17},{17... | collective-permute-start | bytes 12296 | tf_op jit(solution)/shard_map/ppermute | solution.py:22
  207.4 3.9 collective-permute-done.15
  232.5 1.4 fusion.121
  237.6 14.9 %all-to-all-start.2 = ((bf16[128,2,512]{2,1,0:T(2,128)(2,1)}), bf16[128,2,512]{2,1,0:T(2,128)(2,1)S(1)}, u32[]{:S(2)}, u32[]{:S(2)}) async-start(bf16[128,2,512]{2,1,0:T(2,128)(2,1)} %reshape.687), calls=%async_computation.2 | async-start | bytes 524288 | tf_op jit(solution)/shard_map/all_to_all | solution.py:132
  252.7 83.2 %all-reduce.9.cloned.1.call-done = (f32[27,64,64]{2,1,0:T(8,128)}, f32[27,64,64]{2,1,0:T(8,128)}, f32[8,64,64]{2,1,0:T(8,128)}) async-done(((f32[27,64,64]{2,1,0:T(8,128)}, f32[27,64,64]{2,1,0:T(8,128)}, f32[8,64,64]{2,1,0:T(8,128)}), (f32[27,64,64]{2,1,0:T(8,128)}, f32[27,64,64]{2,1,0:T(8,128)}, f32[8,64,64]{2,1,0:T(8,128)})) %all-reduce.9.cloned.1.call-update) | async-done | bytes 1015824 | tf_op jit(solution)/shard_map/psum | solution.py:11
  338.4 65.0 %all-reduce.11.cloned.1.call-done = (f32[27,64,64]{2,1,0:T(8,128)}, f32[27,64,64]{2,1,0:T(8,128)}, f32[8,64,64]{2,1,0:T(8,128)}) async-done(((f32[27,64,64]{2,1,0:T(8,128)}, f32[27,64,64]{2,1,0:T(8,128)}, f32[8,64,64]{2,1,0:T(8,128)}), (f32[27,64,64]{2,1,0:T(8,128)}, f32[27,64,64]{2,1,0:T(8,128)}, f32[8,64,64]{2,1,0:T(8,128)})) %all-reduce.11.cloned.1.call-update) | async-done | bytes 1015824 | tf_op jit(solution)/shard_map/psum | solution.py:12
  403.4 1.7 broadcast_multiply_fusion.2
  405.1 2.9 broadcast_multiply_fusion
  (366 shorter events, 121.3 us)
Async XLA Ops:
  7.2 39.7 %copy-start = (bf16[8,64,64]{2,1,0:T(8,128)(2,1)S(1)}, bf16[8,64,64]{2,1,0:T(8,128)(2,1)}, u32[]{:S(2)}) copy-start(bf16[8,64,64]{2,1,0:T(8,128)(2,1)} %param.11) | copy-start | bytes 196612
  9.8 20.6 %all-to-all-start.1 = ((s32[1,128,16]{2,0,1:T(1,128)}), s32[1,128,16]{2,0,1:T(1,128)S(1)}, u32[]{:S(2)}, u32[]{:S(2)}) async-start(s32[1,128,16]{2,0,1:T(1,128)} %bitcast.3), calls=%async_computation.1 | async-start | bytes 131072 | tf_op jit(solution)/shard_map/all_to_all | solution.py:91
  22.9 12.1 %copy-start.6 = (s32[2,8,128]{2,1,0:T(8,128)S(1)}, s32[2,8,128]{2,1,0:T(8,128)}, u32[]{:S(2)}) copy-start(s32[2,8,128]{2,1,0:T(8,128)} %param.14) | copy-start | bytes 24580
  30.4 15.5 %all-to-all-start = ((bf16[128,2,512]{2,1,0:T(2,128)(2,1)}), bf16[128,2,512]{2,1,0:T(2,128)(2,1)S(1)}, u32[]{:S(2)}, u32[]{:S(2)}) async-start(bf16[128,2,512]{2,1,0:T(2,128)(2,1)} %reshape.685), calls=%async_computation | async-start | bytes 524288 | tf_op jit(solution)/shard_map/all_to_all | solution.py:90
  35.0 300.9 %all-reduce.9.cloned.1.call-start = ((), (), s32[]{:S(2)}) async-start(), calls=%async_computation.3 | async-start | bytes 4063232 | tf_op jit(solution)/shard_map/psum | solution.py:11
  48.6 5.4 %collective-permute-start = (bf16[64,1,8,128]{3,0,2,1:T(8,128)(2,1)S(1)}, bf16[64,1,8,128]{3,0,2,1:T(8,128)(2,1)S(1)}, u32[]{:S(2)}, u32[]{:S(2)}) collective-permute-start(bf16[64,1,8,128]{3,0,2,1:T(8,128)(2,1)S(1)} %get-tuple-element.151), channel_id=1, source_target_pairs={{0,1},{1,2},{2,3},{3,4},{4,5},{5,6},{6,7},{7,8},{8,9},{9,10},{10,1... | collective-permute-start | bytes 393224 | tf_op jit(solution)/shard_map/ppermute | solution.py:22
  51.4 6.9 %collective-permute-start.1 = (bf16[64,1,8,128]{3,0,2,1:T(8,128)(2,1)S(1)}, bf16[64,1,8,128]{3,0,2,1:T(8,128)(2,1)S(1)}, u32[]{:S(2)}, u32[]{:S(2)}) collective-permute-start(bf16[64,1,8,128]{3,0,2,1:T(8,128)(2,1)S(1)} %get-tuple-element.152), channel_id=1, source_target_pairs={{1,0},{2,1},{3,2},{4,3},{5,4},{6,5},{7,6},{8,7},{9,8},{10,9},{11,1... | collective-permute-start | bytes 393224 | tf_op jit(solution)/shard_map/ppermute | solution.py:23
  58.6 4.3 %collective-permute-start.2 = (bf16[64,4,8,1]{3,0,2,1:T(8,128)(2,1)S(1)}, bf16[64,4,8,1]{3,0,2,1:T(8,128)(2,1)S(1)}, u32[]{:S(2)}, u32[]{:S(2)}) collective-permute-start(bf16[64,4,8,1]{3,0,2,1:T(8,128)(2,1)S(1)} %get-tuple-element.135), channel_id=1, source_target_pairs={{0,16},{16,32},{32,48},{48,64},{64,80},{80,96},{96,112},{1,17},{17... | collective-permute-start | bytes 12296 | tf_op jit(solution)/shard_map/ppermute | solution.py:22
  59.9 4.6 %collective-permute-start.3 = (bf16[64,4,8,1]{3,0,2,1:T(8,128)(2,1)S(1)}, bf16[64,4,8,1]{3,0,2,1:T(8,128)(2,1)S(1)}, u32[]{:S(2)}, u32[]{:S(2)}) collective-permute-start(bf16[64,4,8,1]{3,0,2,1:T(8,128)(2,1)S(1)} %get-tuple-element.136), channel_id=1, source_target_pairs={{16,0},{32,16},{48,32},{64,48},{80,64},{96,80},{112,96},{17,1},{33... | collective-permute-start | bytes 12296 | tf_op jit(solution)/shard_map/ppermute | solution.py:23
  69.3 1.0 copy-start.1
  83.8 4.8 %collective-permute-start.4 = (bf16[64,1,8,128]{3,0,2,1:T(8,128)(2,1)S(1)}, bf16[64,1,8,128]{3,0,2,1:T(8,128)(2,1)S(1)}, u32[]{:S(2)}, u32[]{:S(2)}) collective-permute-start(bf16[64,1,8,128]{3,0,2,1:T(8,128)(2,1)S(1)} %get-tuple-element.149), channel_id=1, source_target_pairs={{0,1},{1,2},{2,3},{3,4},{4,5},{5,6},{6,7},{7,8},{8,9},{9,10},{10,1... | collective-permute-start | bytes 393224 | tf_op jit(solution)/shard_map/ppermute | solution.py:22
  86.0 6.9 %collective-permute-start.5 = (bf16[64,1,8,128]{3,0,2,1:T(8,128)(2,1)S(1)}, bf16[64,1,8,128]{3,0,2,1:T(8,128)(2,1)S(1)}, u32[]{:S(2)}, u32[]{:S(2)}) collective-permute-start(bf16[64,1,8,128]{3,0,2,1:T(8,128)(2,1)S(1)} %get-tuple-element.150), channel_id=1, source_target_pairs={{1,0},{2,1},{3,2},{4,3},{5,4},{6,5},{7,6},{8,7},{9,8},{10,9},{11,1... | collective-permute-start | bytes 393224 | tf_op jit(solution)/shard_map/ppermute | solution.py:23
  93.2 9.6 %collective-permute-start.6 = (bf16[64,4,8,1]{3,0,2,1:T(8,128)(2,1)S(1)}, bf16[64,4,8,1]{3,0,2,1:T(8,128)(2,1)S(1)}, u32[]{:S(2)}, u32[]{:S(2)}) collective-permute-start(bf16[64,4,8,1]{3,0,2,1:T(8,128)(2,1)S(1)} %get-tuple-element.133), channel_id=1, source_target_pairs={{0,16},{16,32},{32,48},{48,64},{64,80},{80,96},{96,112},{1,17},{17... | collective-permute-start | bytes 12296 | tf_op jit(solution)/shard_map/ppermute | solution.py:22
  100.9 5.5 %collective-permute-start.7 = (bf16[64,4,8,1]{3,0,2,1:T(8,128)(2,1)S(1)}, bf16[64,4,8,1]{3,0,2,1:T(8,128)(2,1)S(1)}, u32[]{:S(2)}, u32[]{:S(2)}) collective-permute-start(bf16[64,4,8,1]{3,0,2,1:T(8,128)(2,1)S(1)} %get-tuple-element.134), channel_id=1, source_target_pairs={{16,0},{32,16},{48,32},{64,48},{80,64},{96,80},{112,96},{17,1},{33... | collective-permute-start | bytes 12296 | tf_op jit(solution)/shard_map/ppermute | solution.py:23
  111.2 1.0 copy-start.2
  125.6 1.0 copy-start.5
  133.3 8.0 %collective-permute-start.8 = (bf16[64,1,8,128]{3,0,2,1:T(8,128)(2,1)S(1)}, bf16[64,1,8,128]{3,0,2,1:T(8,128)(2,1)S(1)}, u32[]{:S(2)}, u32[]{:S(2)}) collective-permute-start(bf16[64,1,8,128]{3,0,2,1:T(8,128)(2,1)S(1)} %get-tuple-element.147), channel_id=1, source_target_pairs={{0,1},{1,2},{2,3},{3,4},{4,5},{5,6},{6,7},{7,8},{8,9},{9,10},{10,1... | collective-permute-start | bytes 393224 | tf_op jit(solution)/shard_map/ppermute | solution.py:22
  138.8 6.9 %collective-permute-start.9 = (bf16[64,1,8,128]{3,0,2,1:T(8,128)(2,1)S(1)}, bf16[64,1,8,128]{3,0,2,1:T(8,128)(2,1)S(1)}, u32[]{:S(2)}, u32[]{:S(2)}) collective-permute-start(bf16[64,1,8,128]{3,0,2,1:T(8,128)(2,1)S(1)} %get-tuple-element.148), channel_id=1, source_target_pairs={{1,0},{2,1},{3,2},{4,3},{5,4},{6,5},{7,6},{8,7},{9,8},{10,9},{11,1... | collective-permute-start | bytes 393224 | tf_op jit(solution)/shard_map/ppermute | solution.py:23
  146.0 9.5 %collective-permute-start.10 = (bf16[64,4,8,1]{3,0,2,1:T(8,128)(2,1)S(1)}, bf16[64,4,8,1]{3,0,2,1:T(8,128)(2,1)S(1)}, u32[]{:S(2)}, u32[]{:S(2)}) collective-permute-start(bf16[64,4,8,1]{3,0,2,1:T(8,128)(2,1)S(1)} %get-tuple-element.131), channel_id=1, source_target_pairs={{0,16},{16,32},{32,48},{48,64},{64,80},{80,96},{96,112},{1,17},{17... | collective-permute-start | bytes 12296 | tf_op jit(solution)/shard_map/ppermute | solution.py:22
  153.7 5.2 %collective-permute-start.11 = (bf16[64,4,8,1]{3,0,2,1:T(8,128)(2,1)S(1)}, bf16[64,4,8,1]{3,0,2,1:T(8,128)(2,1)S(1)}, u32[]{:S(2)}, u32[]{:S(2)}) collective-permute-start(bf16[64,4,8,1]{3,0,2,1:T(8,128)(2,1)S(1)} %get-tuple-element.132), channel_id=1, source_target_pairs={{16,0},{32,16},{48,32},{64,48},{80,64},{96,80},{112,96},{17,1},{33... | collective-permute-start | bytes 12296 | tf_op jit(solution)/shard_map/ppermute | solution.py:23
  155.3 0.9 copy-start.3
  187.1 6.3 %collective-permute-start.12 = (bf16[64,1,8,128]{3,0,2,1:T(8,128)(2,1)S(1)}, bf16[64,1,8,128]{3,0,2,1:T(8,128)(2,1)S(1)}, u32[]{:S(2)}, u32[]{:S(2)}) collective-permute-start(bf16[64,1,8,128]{3,0,2,1:T(8,128)(2,1)S(1)} %get-tuple-element.145), channel_id=1, source_target_pairs={{0,1},{1,2},{2,3},{3,4},{4,5},{5,6},{6,7},{7,8},{8,9},{9,10},{10,1... | collective-permute-start | bytes 393224 | tf_op jit(solution)/shard_map/ppermute | solution.py:22
  190.9 6.9 %collective-permute-start.13 = (bf16[64,1,8,128]{3,0,2,1:T(8,128)(2,1)S(1)}, bf16[64,1,8,128]{3,0,2,1:T(8,128)(2,1)S(1)}, u32[]{:S(2)}, u32[]{:S(2)}) collective-permute-start(bf16[64,1,8,128]{3,0,2,1:T(8,128)(2,1)S(1)} %get-tuple-element.146), channel_id=1, source_target_pairs={{1,0},{2,1},{3,2},{4,3},{5,4},{6,5},{7,6},{8,7},{9,8},{10,9},{11,1... | collective-permute-start | bytes 393224 | tf_op jit(solution)/shard_map/ppermute | solution.py:23
  198.0 9.3 %collective-permute-start.14 = (bf16[64,4,8,1]{3,0,2,1:T(8,128)(2,1)S(1)}, bf16[64,4,8,1]{3,0,2,1:T(8,128)(2,1)S(1)}, u32[]{:S(2)}, u32[]{:S(2)}) collective-permute-start(bf16[64,4,8,1]{3,0,2,1:T(8,128)(2,1)S(1)} %get-tuple-element.129), channel_id=1, source_target_pairs={{0,16},{16,32},{32,48},{48,64},{64,80},{80,96},{96,112},{1,17},{17... | collective-permute-start | bytes 12296 | tf_op jit(solution)/shard_map/ppermute | solution.py:22
  205.8 5.5 %collective-permute-start.15 = (bf16[64,4,8,1]{3,0,2,1:T(8,128)(2,1)S(1)}, bf16[64,4,8,1]{3,0,2,1:T(8,128)(2,1)S(1)}, u32[]{:S(2)}, u32[]{:S(2)}) collective-permute-start(bf16[64,4,8,1]{3,0,2,1:T(8,128)(2,1)S(1)} %get-tuple-element.130), channel_id=1, source_target_pairs={{16,0},{32,16},{48,32},{64,48},{80,64},{96,80},{112,96},{17,1},{33... | collective-permute-start | bytes 12296 | tf_op jit(solution)/shard_map/ppermute | solution.py:23
  207.3 3.9 copy-start.4
  236.3 16.2 %copy-start.7 = (s32[1,128]{1,0:T(1,128)S(1)}, s32[1,128]{1,0:T(1,128)}, u32[]{:S(2)}) copy-start(s32[1,128]{1,0:T(1,128)} %param.10) | copy-start | bytes 1540
  237.6 99.2 %all-to-all-start.2 = ((bf16[128,2,512]{2,1,0:T(2,128)(2,1)}), bf16[128,2,512]{2,1,0:T(2,128)(2,1)S(1)}, u32[]{:S(2)}, u32[]{:S(2)}) async-start(bf16[128,2,512]{2,1,0:T(2,128)(2,1)} %reshape.687), calls=%async_computation.2 | async-start | bytes 524288 | tf_op jit(solution)/shard_map/all_to_all | solution.py:132
  252.5 150.9 %all-reduce.11.cloned.1.call-start = ((), (), s32[]{:S(2)}) async-start(), calls=%async_computation.4 | async-start | bytes 4063232 | tf_op jit(solution)/shard_map/psum | solution.py:12
Sparse Core Ops, SparseCore 0:
  235.8 100.0 all-reduce.8
  338.4 64.8 all-reduce.10
